TPU v7x, 128 devices: a whole 4x4x4 slice. The times are simulated.
128 devices in a mesh: dp: 8 (over x, core), cent: 16 (over z, y).
Axes of the slice: x: 4, y: 4, z: 4, core: 2. Of those that a mesh axis runs over, the one named last changes fastest.
Arguments:
- points: bfloat16 [131072, 1024], P(('dp', 'cent')), may hold values from -16 to 16
- point_cluster: int32 [131072], P(('dp', 'cent')), may hold values from 0 to 32767, as said below
- cand_blocks: int32 [1024, 8], P(('dp', 'cent')), may hold values from 0 to 31, as said below
- cent1_prev: float32 [32768, 1024], P(('dp', 'cent')), may hold values from -6 to 6
- parent: int32 [32768], P(('dp', 'cent')), may hold values from 0 to 4095, as said below
- cent2_prev: bfloat16 [4096, 1024], P('dp'), may hold values from -6 to 6
Outputs:
- cent1_new: float32 [32768, 1024], P(('dp', 'cent'))
- cent2_new: float32 [4096, 1024], P('dp')
- point_score: float32 [131072], P(('dp', 'cent'))
Inputs may be any that keep to these rules, and one draw needn't show every extreme that they name: All points of an aligned block of 128 points share one level-one block (point_cluster // 128); on a device these block numbers never fall; the points of a device at index i of dp name only centroids from i * 16 * 256 to (i + 1) * 16 * 256 - 1; at most 2 point blocks of one device fall to one owner's 256 centroids, and in every draw one owner in each index of dp receives exactly 2 blocks from every device of that index. `parent`: the level-one centroids held at index i of dp name level-two centroids from i * 512 to (i + 1) * 512 - 1. `cand_blocks`: each row lists 8 different level-two blocks.
All inputs are finite; a program needn't handle non-finite values.
Results may differ from a plain program's by a relative error of at most 0.00094.
Values may be sent and summed in bfloat16 or wider, within the bound.
A program may use at most 128 MiB of HBM per device.

v0:
```python
import jax
import jax.numpy as jnp
from jax import lax
from jax.sharding import PartitionSpec as P

BLOCK = 128


EPSILON = 1e-06
SHARPNESS = 20.0


def rms_norm(values):
    return values * lax.rsqrt(jnp.mean(values * values, axis=-1, keepdims=True) + EPSILON)


def shards(points, point_cluster, cand_blocks, cent1_prev, parent, cent2_prev):
    width = points.shape[1]
    row_count = points.shape[0]
    block_count = row_count // BLOCK
    owned_rows = cent1_prev.shape[0]
    owned_blocks = owned_rows // BLOCK
    n_cent = lax.axis_size("cent")
    unit_points = rms_norm(points.astype(jnp.float32)).astype(jnp.bfloat16)
    point_blocks = points.reshape(block_count, BLOCK, width)
    cluster_blocks = point_cluster.reshape(block_count, BLOCK)
    leading = cluster_blocks[:, 0]
    offsets = cluster_blocks % BLOCK
    member = (offsets[:, :, None] == jnp.arange(BLOCK)[None, None, :]).astype(jnp.bfloat16)
    block_sums = jnp.einsum(
        "bpc,bpd->bcd", member, point_blocks, preferred_element_type=jnp.float32
    )
    block_counts = jnp.sum(member.astype(jnp.float32), axis=1)
    target = leading % (owned_rows * n_cent) // BLOCK
    routing = (target[None, :] == jnp.arange(n_cent * owned_blocks)[:, None]).astype(jnp.float32)
    dense_sums = jnp.dot(
        routing,
        block_sums.reshape(block_count, BLOCK * width),
        precision=lax.Precision.HIGHEST,
        preferred_element_type=jnp.float32,
    ).reshape(n_cent * owned_rows, width)
    dense_counts = jnp.dot(
        routing, block_counts, precision=lax.Precision.HIGHEST, preferred_element_type=jnp.float32
    )
    level_sums, counts = (
        lax.psum_scatter(dense_sums, "cent", scatter_dimension=0, tiled=True),
        lax.psum_scatter(dense_counts, "cent", scatter_dimension=0, tiled=True),
    )
    counts = counts.reshape(owned_rows)
    average = level_sums / jnp.maximum(counts, 1.0)[:, None]
    cent1_new = rms_norm(average + cent1_prev)
    upper_rows = cent2_prev.shape[0]
    parent_local = parent - lax.axis_index("dp") * upper_rows
    membership = (parent_local[None, :] == jnp.arange(upper_rows)[:, None]).astype(jnp.float32)
    upper_part = jnp.dot(
        membership, cent1_new, precision=lax.Precision.HIGHEST, preferred_element_type=jnp.float32
    )
    cent2_new = rms_norm(lax.psum(upper_part, "cent"))
    column_scale = SHARPNESS / width
    table_rows = lax.all_gather(cent2_prev, "dp", axis=0, tiled=True)
    table_units = rms_norm(table_rows.astype(jnp.float32)).astype(jnp.bfloat16)
    products = lax.dot_general(
        unit_points, table_units, (((1,), (1,)), ((), ())), preferred_element_type=jnp.float32
    )
    column_block = jnp.arange(table_rows.shape[0]) // BLOCK
    listed = jnp.any(cand_blocks[:, :, None] == column_block[None, None, :], axis=1)
    weights = jnp.exp(products * column_scale).reshape(block_count, BLOCK, -1) * listed[
        :, None, :
    ].astype(jnp.float32)
    running = jnp.sum(weights, axis=2).reshape(row_count)
    point_score = jnp.log(running)
    return (cent1_new, cent2_new, point_score)


def solution(mesh):
    placed = (
        P(("dp", "cent"), None),
        P(("dp", "cent")),
        P(("dp", "cent"), None),
        P(("dp", "cent"), None),
        P(("dp", "cent")),
        P("dp", None),
    )
    return jax.shard_map(
        shards,
        mesh=mesh,
        in_specs=placed,
        out_specs=(P(("dp", "cent"), None), P("dp", None), P(("dp", "cent"))),
        check_vma=False,
    )
```

profile of v0, /device:TPU:0, one launch (start us, length us, event | category | flops | bytes accessed | tf_op | source)
XLA Modules:
  0.0 259.1 jit_solution(3608974582810143340)
XLA Ops:
  8.0 0.0 reduce-scatter.2.cloned.1.call-start
  8.0 0.7 add_select_fusion.1
  8.7 2.3 convolution_bitcast_fusion
  11.0 0.0 copy-start.4
  11.0 2.4 copy.10
  13.5 0.0 copy-done.4
  13.5 0.1 slice_reduce_fusion
  13.6 9.5 %fusion.16 = f32[32,131072]{1,0:T(8,128)} fusion(f32[8,131072]{1,0:T(8,128)S(1)} %bitcast.17, s32[8]{0:T(128)S(1)} %and_select_fusion), kind=kOutput, calls=%fused_computation.35 | convolution fusion | flops 402653440 | bytes 20971552 | tf_op jit(solution)/shard_map/dot_general | solution.py:36
  23.1 12.1 %reshape.142 = f32[4096,1024]{1,0:T(8,128)} reshape(f32[32,131072]{1,0:T(8,128)} %fusion.16) | data formatting | bytes 33554432 | tf_op jit(solution)/shard_map/reshape | solution.py:41
  35.2 0.0 copy-start.7
  35.2 0.0 copy-start.6
  35.2 0.0 copy-start.2
  35.2 0.0 reduce-scatter.2.cloned.1.call-update
  35.2 0.0 all-gather.2.cloned.1.call-start
  35.3 0.5 all-gather.2.cloned.1.call-update
  35.8 0.0 all-reduce.3.cloned.1.call-start
  35.8 0.0 copy-done.7
  35.8 0.6 dynamic-slice
  37.1 0.1 convert_reduce_fusion
  37.2 0.1 fusion.15
  37.4 78.2 %all-reduce = f32[32,128]{1,0:T(8,128)S(1)} all-reduce(f32[32,128]{1,0:T(8,128)S(1)} %fusion.15), channel_id=3, replica_groups=mesh['dp'=8,'cent'=16] {'cent'}, use_global_device_ids=true, to_apply=%region_2.3.clone | all-reduce | flops 4096 | bytes 32768
  115.6 0.0 copy-done.6
  115.6 34.2 %reduce-scatter.2.cloned.1.call-done = f32[256,1024]{1,0:T(8,128)} async-done(((f32[4096,1024]{1,0:T(8,128)}), f32[256,1024]{1,0:T(8,128)}) %reduce-scatter.2.cloned.1.call-update) | async-done | bytes 1048592 | tf_op jit(solution)/shard_map/reduce_scatter | solution.py:46
  149.8 0.0 copy-done.2
  149.8 1.5 multiply_reduce_fusion.1
  151.3 0.0 copy-start.5
  151.3 0.0 copy-start.1
  151.4 1.6 broadcast_multiply_fusion.1
  152.9 0.0 copy-start.3
  152.9 1.0 copy-done.3
  153.9 2.4 fusion.10
  156.3 0.0 all-reduce.3.cloned.1.call-update
  156.3 0.0 copy-done.5
  156.3 0.4 compare_reduce_fusion
  156.8 0.0 copy-done.1
  156.8 0.5 fusion.5
  157.3 0.0 all-gather.2.cloned.1.call-done
  157.3 0.0 copy-start
  157.3 5.2 %fusion = f32[4096]{0:T(1024)S(1)} fusion(bf16[4096,1024]{1,0:T(8,128)(2,1)} %all-gather.2.cloned.1.call-done), kind=kLoop, calls=%fused_computation.2 | loop fusion | flops 12578816 | bytes 8404992 | tf_op jit(solution)/shard_map/reduce_sum | solution.py:14
  162.6 0.5 copy-done
  163.1 9.8 %fusion.2 = f32[1024]{0:T(1024)S(1)} fusion(bf16[4096,1024]{1,0:T(8,128)(2,1)S(1)} %copy-done, f32[8,4096]{1,0:T(8,128)S(1)} %convert_element_type.34, f32[4096]{0:T(1024)S(1)} %add_rsqrt_fusion, bf16[1024,1024]{1,0:T(8,128)(2,1)S(1)} %copy-done.1, f32[1024]{0:T(1024)S(1)} %add_rsqrt_fusion.1), kind=kOutput, calls=%fused_computation.5 | convolution fusion | flops 8618245120 | bytes 10641408 | tf_op jit(solution)/shard_map/dot_general | solution.py:62
  172.8 0.6 log.3
  173.4 73.2 %all-reduce.3.cloned.1.call-done = f32[512,1024]{1,0:T(8,128)} async-done(((f32[512,1024]{1,0:T(8,128)}), f32[512,1024]{1,0:T(8,128)}) %all-reduce.3.cloned.1.call-update) | async-done | bytes 2097168 | tf_op jit(solution)/shard_map/psum | solution.py:58
  246.7 1.8 multiply_reduce_fusion
  248.5 3.1 %broadcast_multiply_fusion = f32[512,1024]{1,0:T(8,128)} fusion(f32[512,1024]{1,0:T(8,128)} %all-reduce.3.cloned.1.call-done, f32[512]{0:T(512)S(1)} %add_rsqrt_fusion.2), kind=kLoop, calls=%fused_computation.14 | loop fusion | flops 524288 | bytes 4196352 | tf_op jit(solution)/shard_map/mul | solution.py:14
  (9 shorter events, 0.1 us)
Async XLA Ops:
  8.0 141.8 %reduce-scatter.2.cloned.1.call-start = ((), (), s32[]{:S(2)}) async-start(), calls=%async_computation.1 | async-start | bytes 17825792 | tf_op jit(solution)/shard_map/reduce_scatter | solution.py:46
  11.0 2.5 copy-start.4
  35.2 0.7 copy-start.7
  35.2 80.4 %copy-start.6 = (s32[256]{0:T(256)S(1)}, s32[256]{0:T(256)}, u32[]{:S(2)}) copy-start(s32[256]{0:T(256)} %param.10) | copy-start | bytes 3076
  35.2 114.6 %copy-start.2 = (f32[256,1024]{1,0:T(8,128)S(1)}, f32[256,1024]{1,0:T(8,128)}, u32[]{:S(2)}) copy-start(f32[256,1024]{1,0:T(8,128)} %param.9) | copy-start | bytes 3145732
  35.2 122.1 %all-gather.2.cloned.1.call-start = ((), (), s32[]{:S(2)}) async-start(), calls=%async_computation.3 | async-start | bytes 9437184 | tf_op jit(solution)/shard_map/all_gather | solution.py:60
  35.8 210.9 %all-reduce.3.cloned.1.call-start = ((), (), s32[]{:S(2)}) async-start(), calls=%async_computation.2 | async-start | bytes 4194304 | tf_op jit(solution)/shard_map/psum | solution.py:58
  151.3 5.0 %copy-start.5 = (s32[8,8]{1,0:T(8,128)S(1)}, s32[8,8]{1,0:T(8,128)}, u32[]{:S(2)}) copy-start(s32[8,8]{1,0:T(8,128)} %param.8) | copy-start | bytes 772
  151.3 5.4 %copy-start.1 = (bf16[1024,1024]{1,0:T(8,128)(2,1)S(1)}, bf16[1024,1024]{1,0:T(8,128)(2,1)}, u32[]{:S(2)}) copy-start(bf16[1024,1024]{1,0:T(8,128)(2,1)} %param.6) | copy-start | bytes 6291460
  152.9 1.0 copy-start.3
  157.3 5.8 %copy-start = (bf16[4096,1024]{1,0:T(8,128)(2,1)S(1)}, bf16[4096,1024]{1,0:T(8,128)(2,1)}, u32[]{:S(2)}) copy-start(bf16[4096,1024]{1,0:T(8,128)(2,1)} %all-gather.2.cloned.1.call-done) | copy-start | bytes 25165828
Sparse Core Ops, SparseCore 0:
  35.3 114.4 reduce-scatter.1
  156.4 90.2 all-reduce.2
Sparse Core Ops, SparseCore 1:
  37.4 52.0 all-gather.1
where the time goes:
time: 259 us
  waiting for transfers between devices  108 us (42%)
  blocking collectives  78.2 us (30%)
  matrix products  24 us (9%)
  local copies, waits for them, and re-layouts  17.3 us (7%)
  between operations  16.3 us (6%)
  other arithmetic  15 us (6%)
    unnamed x1, blocking collectives  78.2 us
    psum x1, waiting for transfers between devices, shards(): cent2_new = rms_norm(lax.psum(upper_part, 'cent'))  73.2 us
    reduce_scatter x1, waiting for transfers between devices, shards(): lax.psum_scatter(dense_sums, 'cent', scatter_dimension=0, tiled=True)  34.2 us
    reshape x1, local copies, waits for them, and re-layouts, shards(): dense_sums = jnp.dot(routing, block_sums.reshape(block_count, BLOCK * wid...  12.1 us
    dot_general x1, matrix products, shards(): lax.dot_general(unit_points, table_units, (((1,), (1,)), ((), ())), prefe...  9.77 us
    dot_general x1, matrix products, shards(): jnp.dot(routing, block_sums.reshape(block_count, BLOCK * width), precisio...  9.46 us
    reduce_sum x4, other arithmetic, rms_norm(): jnp.mean(values * values, axis=-1, keepdims=True) + EPSILON  9.03 us
  transfers between devices with their start and end apart: 3, of which 2 were waited for; matrix products, arithmetic and copies ran while one was open for 9% of the time, Pallas kernels for 0%

commit v1 on v0

v1 whole, which is shorter than its diff:
```python
import jax
import jax.numpy as jnp
from jax import lax
from jax.experimental import pallas as pl
from jax.experimental.pallas import tpu as pltpu
from jax.sharding import PartitionSpec as P

BLOCK = 128
EPSILON = 1e-06
SHARPNESS = 20.0
RING = 4
MESH = pl.DeviceIdType.MESH
F32 = jnp.float32
BF16 = jnp.bfloat16


def rms_norm(values):
    return values * lax.rsqrt(jnp.mean(values * values, axis=-1, keepdims=True) + EPSILON)


def kernel(
    pts_hbm, ids_hbm, cand_ref, prev_hbm, parent_ref, tab_hbm,
    c1_ref, c2_ref, score_ref,
    pts, units, gathered, raw, table, mask, score_acc, ids_all, onehot, part, part_f, part_q, prev,
    up, up_f, up_q, low, low_f, low_q, send_sem, recv_sem, local_sem,
):
    dp = lax.axis_index("dp")
    cent = lax.axis_index("cent")
    x, core = dp // 2, lax.rem(dp, 2)
    z, y = cent // RING, lax.rem(cent, RING)

    def ring(at, step):
        return lax.rem(at + step + RING, RING)

    def y_at(step):
        return {"cent": z * RING + ring(y, step)}

    def z_at(step):
        return {"cent": ring(z, step) * RING + y}

    def x_at(step):
        return {"dp": ring(x, step) * 2 + core}

    partner = {"dp": x * 2 + 1 - core}
    copies = []

    def send(src, dst, device):
        at = len(copies)
        copy = pltpu.make_async_remote_copy(
            src_ref=src, dst_ref=dst, send_sem=send_sem.at[at], recv_sem=recv_sem.at[at],
            device_id=device, device_id_type=MESH,
        )
        copy.start()
        copies.append(copy)
        return copy

    fetches = [
        pltpu.make_async_copy(tab_hbm, raw, local_sem.at[0]),
        pltpu.make_async_copy(pts_hbm, pts, local_sem.at[1]),
        pltpu.make_async_copy(ids_hbm, ids_all.at[cent], local_sem.at[2]),
        pltpu.make_async_copy(prev_hbm, prev, local_sem.at[3]),
    ]
    for fetch in fetches:
        fetch.start()

    barrier = pltpu.get_barrier_semaphore()
    peers = [y_at(1), y_at(-1), y_at(2), z_at(1), z_at(-1), z_at(2), x_at(1), x_at(-1), partner]
    for peer in peers:
        pl.semaphore_signal(barrier, inc=1, device_id=peer, device_id_type=MESH)
    pl.semaphore_wait(barrier, len(peers))

    half = pts.shape[0] // 2
    wide = pts.shape[1] // 2
    lines = ((y_at, z_at), (z_at, y_at))

    first, last = pl.ds(0, half), pl.ds(half, half)
    moved = []
    for h in range(2):
        cols = pl.ds(h * wide, wide)
        near = lines[h][0]
        moved.append(dict(
            pa=send(pts_hbm.at[first, cols], gathered.at[h, 0, first], near(1)),
            mb=send(pts_hbm.at[last, cols], gathered.at[h, 1, last], near(-1)),
        ))
    id_copies = [send(ids_hbm, ids_all.at[cent], y_at(s)) for s in (1, -1, 2)]
    for h in range(2):
        cols = pl.ds(h * wide, wide)
        near = lines[h][0]
        moved[h].update(
            pb=send(pts_hbm.at[last, cols], gathered.at[h, 0, last], near(1)),
            ma=send(pts_hbm.at[first, cols], gathered.at[h, 1, first], near(-1)),
        )

    rows_t = raw.shape[0]
    top, bottom = pl.ds(0, rows_t // 2), pl.ds(rows_t // 2, rows_t // 2)
    fetches[0].wait()

    def norm_table(i, carry):
        rows = pl.ds(pl.multiple_of(i * 64, 64), 64)
        table[dp, rows] = rms_norm(raw[rows].astype(F32)).astype(BF16)
        return carry

    lax.fori_loop(0, rows_t // 64, norm_table, 0)
    own = table.at[dp]
    tab = dict(
        pa=send(own.at[top], own.at[top], x_at(1)),
        mb=send(own.at[bottom], own.at[bottom], x_at(-1)),
        pb=send(own.at[bottom], own.at[bottom], x_at(1)),
        ma=send(own.at[top], own.at[top], x_at(-1)),
        cp=send(own, own, partner),
    )

    for b in range(pts.shape[0] // BLOCK):
        rows = lax.broadcasted_iota(jnp.int32, (mask.shape[0], mask.shape[1], BLOCK), 0) * mask.shape[1]
        rows = rows + lax.broadcasted_iota(jnp.int32, (mask.shape[0], mask.shape[1], BLOCK), 1)
        hit = jnp.zeros(rows.shape, F32)
        for j in range(cand_ref.shape[1]):
            hit = jnp.where(rows == cand_ref[b, j], 1.0, hit)
        mask[:, :, b * BLOCK:(b + 1) * BLOCK] = hit
    score_acc[...] = jnp.zeros_like(score_acc)

    fetches[1].wait()

    def norm_points(i, carry):
        rows = pl.ds(pl.multiple_of(i * 64, 64), 64)
        units[rows] = rms_norm(pts[rows].astype(F32)).astype(BF16)
        return carry

    lax.fori_loop(0, pts.shape[0] // 64, norm_points, 0)

    def score(slot):
        def step(i, carry):
            at = pl.ds(pl.multiple_of(i * 256, 256), 256)
            dots = lax.dot_general(
                table[slot], units[at], (((1,), (1,)), ((), ())), preferred_element_type=F32
            )
            weights = jnp.exp(dots * (SHARPNESS / pts.shape[1]))
            sums = jnp.sum(weights.reshape(mask.shape[1], BLOCK, 256), axis=1)
            score_acc[:, at] += sums * mask[slot, :, at]
            return carry

        lax.fori_loop(0, pts.shape[0] // 256, step, 0)

    fetches[2].wait()
    for copy in id_copies:
        copy.wait_recv()
    rows_ids = ids_all.at[pl.ds(z * RING, RING)]
    id_copies = [send(rows_ids, rows_ids, z_at(s)) for s in (1, -1, 2)]

    own_rows = part.shape[2]
    group_base = dp * (RING * RING * own_rows)

    def owner_base(h, d):
        at = (ring(z, d) * RING + y) if h == 0 else (z * RING + ring(y, d))
        return group_base + at * own_rows

    def source_at(h, step):
        return (z * RING + ring(y, step)) if h == 0 else (ring(z, step) * RING + y)

    def accumulate(h, step, points, lo, dests, fresh=False):
        ids = ids_all[source_at(h, step), :, lo:lo + half]
        count = len(dests)
        for i, d in enumerate(dests):
            target = lax.broadcasted_iota(jnp.int32, (own_rows, half), 0) + owner_base(h, d)
            onehot[i * own_rows:(i + 1) * own_rows] = jnp.where(target == ids, 1.0, 0.0).astype(BF16)
        sums = jnp.dot(onehot[:count * own_rows], points, preferred_element_type=F32)
        for i, d in enumerate(dests):
            piece = sums[i * own_rows:(i + 1) * own_rows]
            if fresh:
                part[h, d] = piece
            else:
                part[h, d] += piece

    every = (0, 1, 2, 3)
    for h in range(2):
        cols = slice(h * wide, (h + 1) * wide)
        accumulate(h, 0, pts[0:half, cols], 0, every, fresh=True)
        accumulate(h, 0, pts[half:, cols], half, every)
    score(dp)
    for copy in id_copies:
        copy.wait_recv()

    for h in range(2):
        near = lines[h][0]
        moved[h]["pa"].wait_recv()
        moved[h]["fa"] = send(gathered.at[h, 0, first], gathered.at[h, 2, first], near(1))
        moved[h]["mb"].wait_recv()
        moved[h]["fb"] = send(gathered.at[h, 1, last], gathered.at[h, 2, last], near(-1))
    before = table.at[ring(x, -1) * 2 + core]
    after = table.at[ring(x, 1) * 2 + core]
    across = table.at[ring(x, 2) * 2 + core]
    tab["pa"].wait_recv()
    tab["fa"] = send(before.at[top], before.at[top], x_at(1))
    tab["mb"].wait_recv()
    tab["fb"] = send(after.at[bottom], after.at[bottom], x_at(-1))
    for h in range(2):
        accumulate(h, -1, gathered[h, 0, 0:half], 0, every)
        accumulate(h, 1, gathered[h, 1, half:], half, every)
    tab["cp"].wait_recv()
    other = 1 - core
    score(x * 2 + other)

    def count(i, carry):
        target = lax.broadcasted_iota(jnp.int32, (own_rows, BLOCK), 0) + (group_base + cent * own_rows)
        for j in range(ids_all.shape[2] // BLOCK):
            carry = carry + jnp.where(target == ids_all[i, :, j * BLOCK:(j + 1) * BLOCK], 1.0, 0.0)
        return carry

    counts = lax.fori_loop(0, ids_all.shape[0], count, jnp.zeros((own_rows, BLOCK), F32))
    counts = jnp.maximum(jnp.sum(counts, axis=1, keepdims=True), 1.0)

    for h in range(2):
        moved[h]["pb"].wait_recv()
        accumulate(h, -1, gathered[h, 0, half:], half, every)
        moved[h]["ma"].wait_recv()
        accumulate(h, 1, gathered[h, 1, 0:half], 0, every)
    tab["pb"].wait_recv()
    tab["q0"] = send(before, before, partner)
    tab["ma"].wait_recv()
    tab["q1"] = send(after, after, partner)
    score(ring(x, -1) * 2 + core)
    score(ring(x, 1) * 2 + core)
    tab["q0"].wait_recv()
    score(ring(x, -1) * 2 + other)
    tab["q1"].wait_recv()
    score(ring(x, 1) * 2 + other)

    class Scatter:
        def __init__(self, src, f, q, line):
            self.src, self.f, self.q, self.line = src, f, q, line
            self.n = q.shape[1] // 2

        def far(self):
            a, b = pl.ds(0, self.n), pl.ds(self.n, self.n)
            self.c2a = send(self.src(2).at[a], self.f.at[0], self.line(1))
            self.c2b = send(self.src(2).at[b], self.f.at[1], self.line(-1))

        def near(self):
            a, b = pl.ds(0, self.n), pl.ds(self.n, self.n)
            self.c1b = send(self.src(1).at[b], self.q.at[0, b], self.line(1))
            self.c3a = send(self.src(3).at[a], self.q.at[1, a], self.line(-1))

        def forward(self):
            a, b = pl.ds(0, self.n), pl.ds(self.n, self.n)
            self.c2a.wait_recv()
            self.src(1)[a] += self.f[0]
            self.c1a = send(self.src(1).at[a], self.q.at[0, a], self.line(1))
            self.c2b.wait_recv()
            self.src(3)[b] += self.f[1]
            self.c3b = send(self.src(3).at[b], self.q.at[1, b], self.line(-1))

        def wait(self):
            for copy in (self.c1b, self.c3a, self.c1a, self.c3b):
                copy.wait_recv()

    def scatter_part(h):
        return Scatter(lambda d: part.at[h, d], part_f.at[h], part_q.at[h], lines[h][1])

    sums = [scatter_part(h) for h in range(2)]
    for h in range(2):
        moved[h]["fa"].wait_recv()
        accumulate(h, 2, gathered[h, 2, 0:half], 0, (2,))
        moved[h]["fb"].wait_recv()
        accumulate(h, 2, gathered[h, 2, half:], half, (2,))
        sums[h].far()
    for h in range(2):
        accumulate(h, 2, gathered[h, 2, 0:half], 0, (1, 3))
        accumulate(h, 2, gathered[h, 2, half:], half, (1, 3))
        sums[h].near()
    for h in range(2):
        accumulate(h, 2, gathered[h, 2, 0:half], 0, (0,))
        accumulate(h, 2, gathered[h, 2, half:], half, (0,))
    tab["fa"].wait_recv()
    tab["fb"].wait_recv()
    tab["q2"] = send(across, across, partner)
    for h in range(2):
        sums[h].forward()
    score(ring(x, 2) * 2 + core)
    tab["q2"].wait_recv()
    score(ring(x, 2) * 2 + other)
    totals = jnp.sum(score_acc[...], axis=0, keepdims=True)
    for b in range(pts.shape[0] // BLOCK):
        score_ref[b:b + 1, :] = jnp.log(totals[:, b * BLOCK:(b + 1) * BLOCK])
    fetches[3].wait()
    for h in range(2):
        sums[h].wait()
    averages = [(part[h, 0] + part_q[h, 0] + part_q[h, 1]) / counts + prev[:, h * wide:(h + 1) * wide] for h in range(2)]
    squares = sum(jnp.sum(v * v, axis=1, keepdims=True) for v in averages)
    scale = lax.rsqrt(squares / pts.shape[1] + EPSILON)
    for h in range(2):
        c1_ref[:, h * wide:(h + 1) * wide] = averages[h] * scale

    block = up.shape[2]
    sub = block // RING
    local = parent_ref[...] - dp * (RING * block)
    swapped = (
        lax.shift_right_logical(local & (block - 1), 5) * block
        + lax.shift_right_logical(local, 7) * sub
        + (local & (sub - 1))
    )
    places = (local, swapped)
    me = ((z, y), (y, z))
    his, los = [], []
    for h in range(2):
        values = c1_ref[:, h * wide:(h + 1) * wide]
        hi = values.astype(BF16)
        his.append(hi)
        los.append((values - hi.astype(F32)).astype(BF16))

    def upper(h, d):
        target = lax.broadcasted_iota(jnp.int32, (block, own_rows), 0) + ring(me[h][0], d) * block
        pick = jnp.where(target == places[h], 1.0, 0.0).astype(BF16)
        up[h, d] = jnp.dot(pick, his[h], preferred_element_type=F32) + jnp.dot(
            pick, los[h], preferred_element_type=F32
        )

    def scatter_up(h):
        return Scatter(lambda d: up.at[h, d], up_f.at[h], up_q.at[h], lines[h][1])

    ups = [scatter_up(h) for h in range(2)]
    for h in range(2):
        upper(h, 2)
        ups[h].far()
    for h in range(2):
        upper(h, 1)
        upper(h, 3)
        ups[h].near()
    for h in range(2):
        upper(h, 0)
    for h in range(2):
        ups[h].forward()

    def scatter_low(h):
        return Scatter(lambda d: low.at[h, ring(me[h][1], d)], low_f.at[h], low_q.at[h], lines[h][0])

    lows = [scatter_low(h) for h in range(2)]
    for h in range(2):
        ups[h].wait()
        low[h] = (up[h, 0] + up_q[h, 0] + up_q[h, 1]).reshape(RING, sub, wide)
        lows[h].far()
        lows[h].near()
    for h in range(2):
        lows[h].forward()
    values = []
    for h in range(2):
        lows[h].wait()
        values.append(low[h, me[h][1]] + low_q[h, 0] + low_q[h, 1])
    squares = sum(jnp.sum(v * v, axis=1, keepdims=True) for v in values)
    scale = lax.rsqrt(squares / pts.shape[1] + EPSILON)
    for h in range(2):
        c2_ref[z, y, :, h * wide:(h + 1) * wide] = values[h] * scale

    class Gather:
        def __init__(self, place, at, line):
            self.place, self.at, self.line = place, at, line

        def start(self):
            at, place, line = self.at, self.place, self.line
            self.pa = send(place(at, 0), place(at, 0), line(1))
            self.mb = send(place(at, 1), place(at, 1), line(-1))
            self.pb = send(place(at, 1), place(at, 1), line(1))
            self.ma = send(place(at, 0), place(at, 0), line(-1))

        def forward(self):
            at, place, line = self.at, self.place, self.line
            self.pa.wait_recv()
            self.fa = send(place(ring(at, -1), 0), place(ring(at, -1), 0), line(1))
            self.mb.wait_recv()
            self.fb = send(place(ring(at, 1), 1), place(ring(at, 1), 1), line(-1))

        def wait(self):
            for copy in (self.pb, self.ma, self.fa, self.fb):
                copy.wait_recv()

    left, right = pl.ds(0, wide), pl.ds(wide, wide)
    small = [
        Gather(lambda k, s: c2_ref.at[z, k, pl.ds(s * (sub // 2), sub // 2), left], y, y_at),
        Gather(lambda k, s: c2_ref.at[k, y, pl.ds(s * (sub // 2), sub // 2), right], z, z_at),
    ]
    large = [
        Gather(lambda k, s: c2_ref.at[k, pl.ds(2 * s, 2), :, left], z, z_at),
        Gather(lambda k, s: c2_ref.at[pl.ds(2 * s, 2), k, :, right], y, y_at),
    ]
    for g in small:
        g.start()
    for g in small:
        g.forward()
    for g, l in zip(small, large):
        g.wait()
        l.start()
    for l in large:
        l.forward()
    for l in large:
        l.wait()
    for copy in copies:
        copy.wait_send()
    assert len(copies) == N_COPIES


N_COPIES = 88


def shards(points, point_cluster, cand_blocks, cent1_prev, parent, cent2_prev):
    rows, width = points.shape
    wide = width // 2
    owned = cent1_prev.shape[0]
    table_rows = cent2_prev.shape[0]
    n_dp = lax.axis_size("dp")
    n_cent = lax.axis_size("cent")
    block = table_rows // RING
    sub = block // RING
    any_spec = pl.BlockSpec(memory_space=pl.ANY)
    vmem = pl.BlockSpec(memory_space=pltpu.VMEM)
    smem = pl.BlockSpec(memory_space=pltpu.SMEM)
    cent1_new, cent2_new, score = pl.pallas_call(
        kernel,
        out_shape=(
            jax.ShapeDtypeStruct((owned, width), F32),
            jax.ShapeDtypeStruct((RING, RING, sub, width), F32),
            jax.ShapeDtypeStruct((rows // BLOCK, BLOCK), F32),
        ),
        in_specs=[any_spec, any_spec, smem, any_spec, vmem, any_spec],
        out_specs=(vmem, vmem, vmem),
        scratch_shapes=[
            pltpu.VMEM((rows, width), BF16),
            pltpu.VMEM((rows, width), BF16),
            pltpu.VMEM((2, 3, rows, wide), BF16),
            pltpu.VMEM((table_rows, width), BF16),
            pltpu.VMEM((n_dp, table_rows, width), BF16),
            pltpu.VMEM((n_dp, table_rows // BLOCK, rows), F32),
            pltpu.VMEM((table_rows // BLOCK, rows), F32),
            pltpu.VMEM((n_cent, 1, rows), jnp.int32),
            pltpu.VMEM((RING * owned, rows // 2), BF16),
            pltpu.VMEM((2, RING, owned, wide), F32),
            pltpu.VMEM((2, 2, owned // 2, wide), F32),
            pltpu.VMEM((2, 2, owned, wide), F32),
            pltpu.VMEM((owned, width), F32),
            pltpu.VMEM((2, RING, block, wide), F32),
            pltpu.VMEM((2, 2, block // 2, wide), F32),
            pltpu.VMEM((2, 2, block, wide), F32),
            pltpu.VMEM((2, RING, sub, wide), F32),
            pltpu.VMEM((2, 2, sub // 2, wide), F32),
            pltpu.VMEM((2, 2, sub, wide), F32),
            pltpu.SemaphoreType.DMA((N_COPIES,)),
            pltpu.SemaphoreType.DMA((N_COPIES,)),
            pltpu.SemaphoreType.DMA((4,)),
        ],
        compiler_params=pltpu.CompilerParams(
            collective_id=0, has_side_effects=True, vmem_limit_bytes=60 * 1024 * 1024
        ),
    )(
        points,
        point_cluster.reshape(1, rows),
        cand_blocks,
        cent1_prev,
        parent.reshape(1, owned),
        cent2_prev,
    )
    return cent1_new, cent2_new.reshape(table_rows, width), score.reshape(rows)


def solution(mesh):
    placed = (
        P(("dp", "cent"), None),
        P(("dp", "cent")),
        P(("dp", "cent"), None),
        P(("dp", "cent"), None),
        P(("dp", "cent")),
        P("dp", None),
    )
    return jax.shard_map(
        shards,
        mesh=mesh,
        in_specs=placed,
        out_specs=(P(("dp", "cent"), None), P("dp", None), P(("dp", "cent"))),
        check_vma=False,
    )
```

time: 259 us -> 113 us (0.44)
  Pallas kernels: 0 us -> 108 us
  waiting for transfers between devices: 108 us -> 0 us
  blocking collectives: 78.2 us -> 0 us
  matrix products: 24 us -> 0 us
  between operations: 16.3 us -> 0.65 us
  other arithmetic: 15 us -> 0 us
  local copies, waits for them, and re-layouts: 17.3 us -> 4.38 us
    pallas_call x0 -> x1, Pallas kernels: none -> 108 us  [shards(): pl.pallas_call(kernel, out_shape=(jax.ShapeDtypeStruct((owned, width), F3...]
    unnamed x1 -> x0, blocking collectives: 78.2 us -> none
    psum x1 -> x0, waiting for transfers between devices: 73.2 us -> none  [shards(): cent2_new = rms_norm(lax.psum(upper_part, 'cent'))]
    reduce_scatter x1 -> x0, waiting for transfers between devices: 34.2 us -> none  [shards(): lax.psum_scatter(dense_sums, 'cent', scatter_dimension=0, tiled=True)]
    dot_general x5 -> x0, matrix products: 24 us -> none  [the longest x1 9.77 us: shards(): lax.dot_general(unit_points, table_units, (((1,), (1,)), ((), ())), prefe...]
    reshape x1 -> x0, local copies, waits for them, and re-layouts: 12.1 us -> none  [shards(): dense_sums = jnp.dot(routing, block_sums.reshape(block_count, BLOCK * wid...]
    reduce_sum x5 -> x0, other arithmetic: 9.17 us -> none  [the longest x4 9.03 us: rms_norm(): jnp.mean(values * values, axis=-1, keepdims=True) + EPSILON]
    mul x2 -> x0, other arithmetic: 4.68 us -> none  [rms_norm(): values * lax.rsqrt(jnp.mean(values * values, axis=-1, keepdims=True) + EP...]
  transfers between devices with their start and end apart: 3 -> 0, of which waited for: 2 -> 0; matrix products, arithmetic and copies ran while one was open for 9% -> 0% of each run, Pallas kernels for 0% -> 0%
where the time goes in v1:
time: 113 us
  Pallas kernels  108 us (96%)
  local copies, waits for them, and re-layouts  4.38 us (4%)
    pallas_call x1, Pallas kernels, shards(): pl.pallas_call(kernel, out_shape=(jax.ShapeDtypeStruct((owned, width), F3...  108 us
    unnamed x7, local copies, waits for them, and re-layouts  4.38 us

profile of v1, /device:TPU:0, one launch (start us, length us, event | category | flops | bytes accessed | tf_op | source)
XLA Modules:
  0.0 113.0 jit_solution(12654121163310233662)
XLA Ops:
  0.6 108.0 %shard_map.85 = (f32[256,1024]{1,0:T(8,128)}, f32[4,4,32,1024]{3,2,1,0:T(8,128)}, f32[8,128]{1,0:T(8,128)}) custom-call(bf16[1024,1024]{1,0:T(8,128)(2,1)} %pts_hbm.1, s32[1,1024]{1,0:T(1,128)} %bitcast.5, s32[8,8]{1,0:T(8,128)} %cand_ref.1, f32[256,1024]{1,0:T(8,128)} %prev_hbm.1, s32[1,256]{1,0:T(1,128)} %bitcast.7, bf16[512,1024]{1,0:T(8,128)(2,1)} %tab_hbm.1), custom_call_target="tpu_custom_call" | custom-call | tf_op jit(solution)/shard_map/pallas_call | solution.py:415
  108.6 0.0 copy-start
  108.7 2.5 %copy.12 = f32[256,1024]{1,0:T(8,128)} copy(f32[256,1024]{1,0:T(8,128)} %get-tuple-element.12) | data formatting | bytes 2097152
  111.1 0.0 copy-done
  111.1 0.0 copy-start.1
  111.1 1.3 %copy.13 = f32[512,1024]{1,0:T(8,128)} copy(f32[512,1024]{1,0:T(8,128)S(1)} %bitcast.4) | data formatting | bytes 4194304
  112.4 0.0 copy-done.1
  112.4 0.6 copy.14
Async XLA Ops:
  108.6 2.5 %copy-start = (f32[4,4,32,1024]{3,2,1,0:T(8,128)S(1)}, f32[4,4,32,1024]{3,2,1,0:T(8,128)}, u32[]{:S(2)}) copy-start(f32[4,4,32,1024]{3,2,1,0:T(8,128)} %get-tuple-element.7) | copy-start | bytes 6291460
  111.1 1.3 %copy-start.1 = (f32[8,128]{1,0:T(8,128)S(1)}, f32[8,128]{1,0:T(8,128)}, u32[]{:S(2)}) copy-start(f32[8,128]{1,0:T(8,128)} %get-tuple-element.8) | copy-start | bytes 12292

commit v2 on v1

v2 whole, which is shorter than its diff:
```python
import jax
import jax.numpy as jnp
from jax import lax
from jax.experimental import pallas as pl
from jax.experimental.pallas import tpu as pltpu
from jax.sharding import PartitionSpec as P

BLOCK = 128
EPSILON = 1e-06
SHARPNESS = 20.0
RING = 4
MESH = pl.DeviceIdType.MESH
F32 = jnp.float32
BF16 = jnp.bfloat16


def rms_norm(values):
    return values * lax.rsqrt(jnp.mean(values * values, axis=-1, keepdims=True) + EPSILON)


def kernel(
    pts_hbm, ids_hbm, cand_hbm, prev_hbm, parent_hbm, tab_hbm,
    c1_ref, c2_ref, score_ref,
    pts, units, gathered, raw, table, mask, score_acc, ids_all, onehot, across_hot, picks, part, part_f, part_q, prev,
    up, up_f, up_q, low, low_f, low_q, cand_ref, parent_ref, send_sem, recv_sem, local_sem,
):
    dp = lax.axis_index("dp")
    cent = lax.axis_index("cent")
    x, core = dp // 2, lax.rem(dp, 2)
    z, y = cent // RING, lax.rem(cent, RING)

    def ring(at, step):
        return lax.rem(at + step + RING, RING)

    def y_at(step):
        return {"cent": z * RING + ring(y, step)}

    def z_at(step):
        return {"cent": ring(z, step) * RING + y}

    def x_at(step):
        return {"dp": ring(x, step) * 2 + core}

    partner = {"dp": x * 2 + 1 - core}
    copies, pending = [], []

    def send(src, dst, device):
        at = len(copies)
        copy = pltpu.make_async_remote_copy(
            src_ref=src, dst_ref=dst, send_sem=send_sem.at[at], recv_sem=recv_sem.at[at],
            device_id=device, device_id_type=MESH,
        )
        copy.start()
        copies.append(copy)
        pending.append(copy)
        return copy

    def sent(copy):
        copy.wait_send()
        pending[:] = [other for other in pending if other is not copy]

    fetches = [
        pltpu.make_async_copy(tab_hbm, raw, local_sem.at[0]),
        pltpu.make_async_copy(pts_hbm, pts, local_sem.at[1]),
        pltpu.make_async_copy(ids_hbm, ids_all.at[cent], local_sem.at[2]),
        pltpu.make_async_copy(prev_hbm, prev, local_sem.at[3]),
        pltpu.make_async_copy(cand_hbm, cand_ref, local_sem.at[4]),
        pltpu.make_async_copy(parent_hbm, parent_ref, local_sem.at[5]),
    ]
    for fetch in fetches:
        fetch.start()

    barrier = pltpu.get_barrier_semaphore()
    peers = [y_at(1), y_at(-1), z_at(1), z_at(-1), x_at(1), x_at(-1), partner]
    for peer in peers:
        pl.semaphore_signal(barrier, inc=1, device_id=peer, device_id_type=MESH)
    pl.semaphore_wait(barrier, len(peers))

    half = pts.shape[0] // 2
    wide = pts.shape[1] // 2
    part_w = wide // 2
    lines = ((y_at, z_at), (z_at, y_at))

    first, last = pl.ds(0, half), pl.ds(half, half)
    moved = []
    for h in range(2):
        cols = pl.ds(h * wide, wide)
        near = lines[h][0]
        moved.append(dict(
            pa=send(pts_hbm.at[first, cols], gathered.at[h, 0, first], near(1)),
            mb=send(pts_hbm.at[last, cols], gathered.at[h, 1, last], near(-1)),
        ))
    id_near = [send(ids_hbm, ids_all.at[cent], y_at(1)), send(ids_hbm, ids_all.at[cent], y_at(-1))]

    rows_t = raw.shape[0]
    top, bottom = pl.ds(0, rows_t // 2), pl.ds(rows_t // 2, rows_t // 2)
    fetches[0].wait()

    def norm_table(i, carry):
        rows = pl.ds(pl.multiple_of(i * 64, 64), 64)
        table[dp, rows] = rms_norm(raw[rows].astype(F32)).astype(BF16)
        return carry

    lax.fori_loop(0, rows_t // 64, norm_table, 0)
    own = table.at[dp]
    tab = dict(
        pa=send(own.at[top], own.at[top], x_at(1)),
        mb=send(own.at[bottom], own.at[bottom], x_at(-1)),
        cp=send(own, own, partner),
    )

    fetches[4].wait()
    fetches[5].wait()
    for b in range(pts.shape[0] // BLOCK):
        rows = lax.broadcasted_iota(jnp.int32, (mask.shape[0], mask.shape[1], BLOCK), 0) * mask.shape[1]
        rows = rows + lax.broadcasted_iota(jnp.int32, (mask.shape[0], mask.shape[1], BLOCK), 1)
        hit = jnp.zeros(rows.shape, F32)
        for j in range(cand_ref.shape[1]):
            hit = jnp.where(rows == cand_ref[b, j], 1.0, hit)
        mask[:, :, b * BLOCK:(b + 1) * BLOCK] = hit
    score_acc[...] = jnp.zeros_like(score_acc)

    fetches[1].wait()

    def norm_points(i, carry):
        rows = pl.ds(pl.multiple_of(i * 64, 64), 64)
        units[rows] = rms_norm(pts[rows].astype(F32)).astype(BF16)
        return carry

    lax.fori_loop(0, pts.shape[0] // 64, norm_points, 0)

    for h in range(2):
        cols = pl.ds(h * wide, wide)
        near = lines[h][0]
        moved[h].update(
            pb=send(pts_hbm.at[last, cols], gathered.at[h, 0, last], near(1)),
            ma=send(pts_hbm.at[first, cols], gathered.at[h, 1, first], near(-1)),
        )
    tab.update(
        pb=send(own.at[bottom], own.at[bottom], x_at(1)),
        ma=send(own.at[top], own.at[top], x_at(-1)),
    )

    def score(slot):
        def step(i, carry):
            at = pl.ds(pl.multiple_of(i * 256, 256), 256)
            dots = lax.dot_general(
                table[slot], units[at], (((1,), (1,)), ((), ())), preferred_element_type=F32
            )
            weights = jnp.exp(dots * (SHARPNESS / pts.shape[1]))
            sums = jnp.sum(weights.reshape(mask.shape[1], BLOCK, 256), axis=1)
            score_acc[:, at] += sums * mask[slot, :, at]
            return carry

        lax.fori_loop(0, pts.shape[0] // 256, step, 0)

    fetches[2].wait()
    for copy in id_near:
        copy.wait_recv()
    passed_ids = ids_all.at[z * RING + ring(y, -1)]
    id_far = send(passed_ids, passed_ids, y_at(1))

    own_rows = part.shape[2]
    group_base = dp * (RING * RING * own_rows)

    def owner_base(h, d):
        at = (ring(z, d) * RING + y) if h == 0 else (z * RING + ring(y, d))
        return group_base + at * own_rows

    def source_at(h, step):
        return (z * RING + ring(y, step)) if h == 0 else (ring(z, step) * RING + y)

    def accumulate(h, step, points, lo, fresh=False):
        ids = ids_all[source_at(h, step), :, lo:lo + half]
        for d in range(RING):
            target = lax.broadcasted_iota(jnp.int32, (own_rows, half), 0) + owner_base(h, d)
            onehot[d * own_rows:(d + 1) * own_rows] = jnp.where(target == ids, 1.0, 0.0).astype(BF16)
        sums = jnp.dot(onehot[...], points, preferred_element_type=F32)
        for d in range(RING):
            for k in range(2):
                piece = sums[d * own_rows:(d + 1) * own_rows, k * part_w:(k + 1) * part_w]
                if fresh:
                    part[2 * k + h, d] = piece
                else:
                    part[2 * k + h, d] += piece

    def prepare(h):
        ids = ids_all[source_at(h, 2)]
        for d in range(RING):
            target = lax.broadcasted_iota(jnp.int32, (own_rows, 2 * half), 0) + owner_base(h, d)
            across_hot[h, d] = jnp.where(target == ids, 1.0, 0.0).astype(BF16)

    def finish(h, k, d):
        part[2 * k + h, d] += jnp.dot(
            across_hot[h, d], gathered[h, 2, :, k * part_w:(k + 1) * part_w], preferred_element_type=F32
        )

    cols = slice(0, wide), slice(wide, 2 * wide)
    accumulate(0, 0, pts[0:half, cols[0]], 0, fresh=True)
    accumulate(0, 0, pts[half:, cols[0]], half)
    id_far.wait_recv()
    rows_ids = ids_all.at[pl.ds(z * RING, RING)]
    id_near = [send(rows_ids, rows_ids, z_at(1)), send(rows_ids, rows_ids, z_at(-1))]
    score(dp)
    tab["cp"].wait_recv()
    other = 1 - core
    score(x * 2 + other)
    for copy in id_near:
        copy.wait_recv()
    passed_ids = ids_all.at[pl.ds(ring(z, -1) * RING, RING)]
    id_far = send(passed_ids, passed_ids, z_at(1))
    accumulate(1, 0, pts[0:half, cols[1]], 0, fresh=True)
    accumulate(1, 0, pts[half:, cols[1]], half)

    def pass_points(h, k):
        near = lines[h][0]
        cols = pl.ds(k * part_w, part_w)
        moved[h]["fa", k] = send(gathered.at[h, 0, first, cols], gathered.at[h, 2, first, cols], near(1))
        moved[h]["fb", k] = send(gathered.at[h, 1, last, cols], gathered.at[h, 2, last, cols], near(-1))

    for h in range(2):
        moved[h]["pa"].wait_recv()
        moved[h]["mb"].wait_recv()
        pass_points(h, 0)
    before = table.at[ring(x, -1) * 2 + core]
    after = table.at[ring(x, 1) * 2 + core]
    across = table.at[ring(x, 2) * 2 + core]
    for h in range(2):
        accumulate(h, -1, gathered[h, 0, 0:half], 0)
        accumulate(h, 1, gathered[h, 1, half:], half)
    for h in range(2):
        pass_points(h, 1)
    tab["pa"].wait_recv()
    tab["fa"] = send(before.at[top], before.at[top], x_at(1))
    tab["mb"].wait_recv()
    tab["fb"] = send(after.at[bottom], after.at[bottom], x_at(-1))
    id_far.wait_recv()

    def count(i, carry):
        target = lax.broadcasted_iota(jnp.int32, (own_rows, BLOCK), 0) + (group_base + cent * own_rows)
        for j in range(ids_all.shape[2] // BLOCK):
            carry = carry + jnp.where(target == ids_all[i, :, j * BLOCK:(j + 1) * BLOCK], 1.0, 0.0)
        return carry

    counts = lax.fori_loop(0, ids_all.shape[0], count, jnp.zeros((own_rows, BLOCK), F32))
    counts = jnp.maximum(jnp.sum(counts, axis=1, keepdims=True), 1.0)

    inverse = 1.0 / counts
    block = up.shape[2]
    sub = block // RING
    local = parent_ref[...] - dp * (RING * block)
    swapped = (
        lax.shift_right_logical(local & (block - 1), 5) * block
        + lax.shift_right_logical(local, 7) * sub
        + (local & (sub - 1))
    )
    places = (local, swapped)
    me = ((z, y), (y, z))
    for h in range(2):
        prepare(h)
        for d in range(RING):
            target = lax.broadcasted_iota(jnp.int32, (block, own_rows), 0) + ring(me[h][0], d) * block
            picks[h, d] = jnp.where(target == places[h], 1.0, 0.0).astype(BF16)

    for h in range(2):
        moved[h]["pb"].wait_recv()
        accumulate(h, -1, gathered[h, 0, half:], half)
        moved[h]["ma"].wait_recv()
        accumulate(h, 1, gathered[h, 1, 0:half], 0)
    tab["pb"].wait_recv()
    tab["q0"] = send(before, before, partner)
    tab["ma"].wait_recv()
    tab["q1"] = send(after, after, partner)

    class Scatter:
        def __init__(self, src, f, q, line):
            self.src, self.f, self.q, self.line = src, f, q, line
            self.n = q.shape[1] // 2

        def far(self):
            a, b = pl.ds(0, self.n), pl.ds(self.n, self.n)
            self.c2a = send(self.src(2).at[a], self.f.at[0], self.line(1))
            self.c2b = send(self.src(2).at[b], self.f.at[1], self.line(-1))

        def left(self):
            sent(self.c2a)
            sent(self.c2b)

        def near(self):
            a, b = pl.ds(0, self.n), pl.ds(self.n, self.n)
            self.c1b = send(self.src(1).at[b], self.q.at[0, b], self.line(1))
            self.c3a = send(self.src(3).at[a], self.q.at[1, a], self.line(-1))

        def forward(self):
            a, b = pl.ds(0, self.n), pl.ds(self.n, self.n)
            self.c2a.wait_recv()
            self.src(1)[a] += self.f[0]
            self.c1a = send(self.src(1).at[a], self.q.at[0, a], self.line(1))
            self.c2b.wait_recv()
            self.src(3)[b] += self.f[1]
            self.c3b = send(self.src(3).at[b], self.q.at[1, b], self.line(-1))

        def wait(self):
            for copy in (self.c1b, self.c3a, self.c1a, self.c3b):
                copy.wait_recv()

    def scatter(src, f, q, stage):
        return [Scatter(lambda d, g=g: src(g, d), f.at[g], q.at[g], lines[g % 2][stage]) for g in range(4)]

    def columns(g):
        at = (g % 2) * wide + (g // 2) * part_w
        return slice(at, at + part_w)

    sums = scatter(lambda g, d: part.at[g, d], part_f, part_q, 1)
    for k in range(2):
        for h in range(2):
            moved[h]["fa", k].wait_recv()
            moved[h]["fb", k].wait_recv()
            finish(h, k, 2)
            sums[2 * k + h].far()
        for h in range(2):
            finish(h, k, 1)
            finish(h, k, 3)
            if k == 0:
                sums[h].near()
        for h in range(2):
            finish(h, k, 0)
        score(ring(x, -1 + 2 * k) * 2 + core)
    sums[2].near()
    sums[3].near()
    sums[0].forward()
    sums[1].forward()
    tab["fa"].wait_recv()
    tab["fb"].wait_recv()
    tab["q2"] = send(across, across, partner)
    tab["q0"].wait_recv()
    score(ring(x, -1) * 2 + other)
    sums[2].forward()
    sums[3].forward()
    tab["q1"].wait_recv()
    score(ring(x, 1) * 2 + other)
    score(ring(x, 2) * 2 + core)
    tab["q2"].wait_recv()
    fetches[3].wait()
    squares = jnp.zeros((own_rows, 1), F32)
    for g in range(4):
        sums[g].wait()
        values = (part[g, 0] + part_q[g, 0] + part_q[g, 1]) * inverse + prev[:, columns(g)]
        c1_ref[:, columns(g)] = values
        squares = squares + jnp.sum(values * values, axis=1, keepdims=True)
    scale = lax.rsqrt(squares / pts.shape[1] + EPSILON)

    his, los = [], []
    for g in range(4):
        values = c1_ref[:, columns(g)] * scale
        c1_ref[:, columns(g)] = values
        hi = values.astype(BF16)
        his.append(hi)
        los.append((values - hi.astype(F32)).astype(BF16))

    def upper(g, d):
        pick = picks[g % 2, d]
        up[g, d] = jnp.dot(pick, his[g], preferred_element_type=F32) + jnp.dot(
            pick, los[g], preferred_element_type=F32
        )

    ups = scatter(lambda g, d: up.at[g, d], up_f, up_q, 1)
    for g in range(4):
        upper(g, 2)
        ups[g].far()
    for g in range(4):
        upper(g, 1)
        upper(g, 3)
    for g in range(4):
        ups[g].left()
        ups[g].near()
    for g in range(4):
        upper(g, 0)
    for g in range(4):
        ups[g].forward()
    score(ring(x, 2) * 2 + other)
    totals = jnp.sum(score_acc[...], axis=0, keepdims=True)
    for b in range(pts.shape[0] // BLOCK):
        score_ref[b:b + 1, :] = jnp.log(totals[:, b * BLOCK:(b + 1) * BLOCK])
    lows = scatter(lambda g, d: low.at[g, ring(me[g % 2][1], d)], low_f, low_q, 0)
    for g in range(4):
        ups[g].wait()
        low[g] = (up[g, 0] + up_q[g, 0] + up_q[g, 1]).reshape(RING, sub, part_w)
        lows[g].far()
        lows[g].near()
    for g in range(4):
        lows[g].forward()
    squares = jnp.zeros((sub, 1), F32)
    values = []
    for g in range(4):
        lows[g].wait()
        values.append(low[g, me[g % 2][1]] + low_q[g, 0] + low_q[g, 1])
        squares = squares + jnp.sum(values[g] * values[g], axis=1, keepdims=True)
    scale = lax.rsqrt(squares / pts.shape[1] + EPSILON)
    for g in range(4):
        c2_ref[z, y, :, columns(g)] = values[g] * scale

    def piece(h, i, j, rows=pl.ds(0, sub)):
        at = (i, j) if h == 0 else (j, i)
        return c2_ref.at[at[0], at[1], rows, pl.ds(h * wide, wide)]

    upper_half, lower_half = pl.ds(0, sub // 2), pl.ds(sub // 2, sub // 2)

    def spread(h, i, j, line):
        src = piece(h, i, j)
        return send(src, src, line(1)), send(src, src, line(-1))

    def pass_on(pair, low_src, high_src, line):
        pair[0].wait_recv()
        first_copy = send(low_src, low_src, line(1))
        pair[1].wait_recv()
        return first_copy, send(high_src, high_src, line(-1))

    def pass_far(h, j, pair):
        i = me[h][0]
        return pass_on(
            pair, piece(h, ring(i, -1), j, upper_half), piece(h, ring(i, 1), j, lower_half), lines[h][1]
        )

    near_pairs, far_pairs, passed = [], [], []
    for h in range(2):
        i, j = me[h]
        near_pairs.append(spread(h, i, j, lines[h][0]))
    for h in range(2):
        for copy in near_pairs[h]:
            sent(copy)
    for h in range(2):
        i, j = me[h]
        far_pairs.append({0: spread(h, i, j, lines[h][1])})
    crossed = []
    for h in range(2):
        i, j = me[h]
        crossed.append(pass_on(
            near_pairs[h], piece(h, i, ring(j, -1), upper_half), piece(h, i, ring(j, 1), lower_half), lines[h][0]
        ))
    for h in range(2):
        i, j = me[h]
        far_pairs[h][-1] = spread(h, i, ring(j, -1), lines[h][1])
        far_pairs[h][1] = spread(h, i, ring(j, 1), lines[h][1])
    for h in range(2):
        passed.append(pass_far(h, me[h][1], far_pairs[h][0]))
    for h in range(2):
        i, j = me[h]
        for copy in crossed[h]:
            copy.wait_recv()
        far_pairs[h][2] = spread(h, i, ring(j, 2), lines[h][1])
    for step in (-1, 1, 2):
        for h in range(2):
            passed.append(pass_far(h, ring(me[h][1], step), far_pairs[h][step]))
    for pair in passed:
        for copy in pair:
            copy.wait_recv()
    for copy in pending:
        copy.wait_send()
    assert len(copies) == N_COPIES


N_COPIES = 144


def shards(points, point_cluster, cand_blocks, cent1_prev, parent, cent2_prev):
    rows, width = points.shape
    wide = width // 2
    owned = cent1_prev.shape[0]
    table_rows = cent2_prev.shape[0]
    n_dp = lax.axis_size("dp")
    n_cent = lax.axis_size("cent")
    block = table_rows // RING
    sub = block // RING
    hbm = pl.BlockSpec(memory_space=pltpu.HBM)
    vmem = pl.BlockSpec(memory_space=pltpu.VMEM)
    cent1_new, cent2_new, score = pl.pallas_call(
        kernel,
        out_shape=(
            jax.ShapeDtypeStruct((owned, width), F32),
            jax.ShapeDtypeStruct((RING, RING, sub, width), F32),
            jax.ShapeDtypeStruct((rows // BLOCK, BLOCK), F32),
        ),
        in_specs=[hbm] * 6,
        out_specs=(vmem, vmem, vmem),
        scratch_shapes=[
            pltpu.VMEM((rows, width), BF16),
            pltpu.VMEM((rows, width), BF16),
            pltpu.VMEM((2, 3, rows, wide), BF16),
            pltpu.VMEM((table_rows, width), BF16),
            pltpu.VMEM((n_dp, table_rows, width), BF16),
            pltpu.VMEM((n_dp, table_rows // BLOCK, rows), F32),
            pltpu.VMEM((table_rows // BLOCK, rows), F32),
            pltpu.VMEM((n_cent, 1, rows), jnp.int32),
            pltpu.VMEM((RING * owned, rows // 2), BF16),
            pltpu.VMEM((2, RING, owned, rows), BF16),
            pltpu.VMEM((2, RING, block, owned), BF16),
            pltpu.VMEM((4, RING, owned, wide // 2), F32),
            pltpu.VMEM((4, 2, owned // 2, wide // 2), F32),
            pltpu.VMEM((4, 2, owned, wide // 2), F32),
            pltpu.VMEM((owned, width), F32),
            pltpu.VMEM((4, RING, block, wide // 2), F32),
            pltpu.VMEM((4, 2, block // 2, wide // 2), F32),
            pltpu.VMEM((4, 2, block, wide // 2), F32),
            pltpu.VMEM((4, RING, sub, wide // 2), F32),
            pltpu.VMEM((4, 2, sub // 2, wide // 2), F32),
            pltpu.VMEM((4, 2, sub, wide // 2), F32),
            pltpu.SMEM(cand_blocks.shape, jnp.int32),
            pltpu.VMEM((1, owned), jnp.int32),
            pltpu.SemaphoreType.DMA((N_COPIES,)),
            pltpu.SemaphoreType.DMA((N_COPIES,)),
            pltpu.SemaphoreType.DMA((6,)),
        ],
        compiler_params=pltpu.CompilerParams(
            collective_id=0, has_side_effects=True, vmem_limit_bytes=44 * 1024 * 1024
        ),
    )(
        pltpu.with_memory_space_constraint(points, pltpu.HBM),
        pltpu.with_memory_space_constraint(point_cluster.reshape(1, rows), pltpu.HBM),
        pltpu.with_memory_space_constraint(cand_blocks, pltpu.HBM),
        pltpu.with_memory_space_constraint(cent1_prev, pltpu.HBM),
        pltpu.with_memory_space_constraint(parent.reshape(1, owned), pltpu.HBM),
        pltpu.with_memory_space_constraint(cent2_prev, pltpu.HBM),
    )
    return cent1_new, cent2_new.reshape(table_rows, width), score.reshape(rows)


def solution(mesh):
    placed = (
        P(("dp", "cent"), None),
        P(("dp", "cent")),
        P(("dp", "cent"), None),
        P(("dp", "cent"), None),
        P(("dp", "cent")),
        P("dp", None),
    )
    return jax.shard_map(
        shards,
        mesh=mesh,
        in_specs=placed,
        out_specs=(P(("dp", "cent"), None), P("dp", None), P(("dp", "cent"))),
        check_vma=False,
    )
```

time: 113 us -> 105 us (0.929)
  Pallas kernels: 108 us -> 102 us
  local copies, waits for them, and re-layouts: 4.38 us -> 2.88 us
    pallas_call x1, Pallas kernels: 108 us -> 102 us  [shards(): pl.pallas_call(kernel, out_shape=(jax.ShapeDtypeStruct((owned, width), F3...]
    unnamed x7 -> x3, local copies, waits for them, and re-layouts: 4.38 us -> 2.88 us
where the time goes in v2:
time: 105 us
  Pallas kernels  102 us (97%)
  local copies, waits for them, and re-layouts  2.88 us (3%)
    pallas_call x1, Pallas kernels, shards(): pl.pallas_call(kernel, out_shape=(jax.ShapeDtypeStruct((owned, width), F3...  102 us
    unnamed x3, local copies, waits for them, and re-layouts  2.88 us

profile of v2, /device:TPU:0, one launch (start us, length us, event | category | flops | bytes accessed | tf_op | source)
XLA Modules:
  0.0 105.3 jit_solution(8530450967380111897)
XLA Ops:
  0.6 101.8 %shard_map.85 = (f32[256,1024]{1,0:T(8,128)S(1)}, f32[4,4,32,1024]{3,2,1,0:T(8,128)S(1)}, f32[8,128]{1,0:T(8,128)S(1)}) custom-call(bf16[1024,1024]{1,0:T(8,128)(2,1)} %pts_hbm.1, s32[1,1024]{1,0:T(1,128)} %bitcast.6, s32[8,8]{1,0:T(8,128)} %cand_hbm.1, f32[256,1024]{1,0:T(8,128)} %prev_hbm.1, s32[1,256]{1,0:T(1,128)} %bitcast.7, bf16[512,1024]{1,0:T(8,128)(2,1)} %tab_hbm.1), custom_call_target="tpu_custom_call" | custom-call | tf_op jit(solution)/shard_map/pallas_call | solution.py:477
  102.4 1.0 copy.12
  103.4 1.3 %copy.13 = f32[512,1024]{1,0:T(8,128)} copy(f32[512,1024]{1,0:T(8,128)S(1)} %bitcast.4) | data formatting | bytes 4194304
  104.7 0.6 copy.14

commit v3 on v2

--- a/solution.py
+++ b/solution.py
@@ -22,7 +22,7 @@
     pts_hbm, ids_hbm, cand_hbm, prev_hbm, parent_hbm, tab_hbm,
     c1_ref, c2_ref, score_ref,
     pts, units, gathered, raw, table, mask, score_acc, ids_all, onehot, across_hot, picks, part, part_f, part_q, prev,
-    up, up_f, up_q, low, low_f, low_q, cand_ref, parent_ref, send_sem, recv_sem, local_sem,
+    up, up_f, up_q, low, low_f, low_q, column_ids, cand_ref, parent_ref, send_sem, recv_sem, local_sem,
 ):
     dp = lax.axis_index("dp")
     cent = lax.axis_index("cent")
@@ -42,7 +42,7 @@
         return {"dp": ring(x, step) * 2 + core}
 
     partner = {"dp": x * 2 + 1 - core}
-    copies, pending = [], []
+    copies = []
 
     def send(src, dst, device):
         at = len(copies)
@@ -52,12 +52,7 @@
         )
         copy.start()
         copies.append(copy)
-        pending.append(copy)
         return copy
-
-    def sent(copy):
-        copy.wait_send()
-        pending[:] = [other for other in pending if other is not copy]
 
     fetches = [
         pltpu.make_async_copy(tab_hbm, raw, local_sem.at[0]),
@@ -81,6 +76,9 @@
     part_w = wide // 2
     lines = ((y_at, z_at), (z_at, y_at))
 
+    row_near = [send(ids_hbm, ids_all.at[cent], y_at(1)), send(ids_hbm, ids_all.at[cent], y_at(-1))]
+    column_near = [send(ids_hbm, column_ids.at[0], z_at(1)), send(ids_hbm, column_ids.at[1], z_at(-1))]
+
     first, last = pl.ds(0, half), pl.ds(half, half)
     moved = []
     for h in range(2):
@@ -90,8 +88,6 @@
             pa=send(pts_hbm.at[first, cols], gathered.at[h, 0, first], near(1)),
             mb=send(pts_hbm.at[last, cols], gathered.at[h, 1, last], near(-1)),
         ))
-    id_near = [send(ids_hbm, ids_all.at[cent], y_at(1)), send(ids_hbm, ids_all.at[cent], y_at(-1))]
-
     rows_t = raw.shape[0]
     top, bottom = pl.ds(0, rows_t // 2), pl.ds(rows_t // 2, rows_t // 2)
     fetches[0].wait()
@@ -107,6 +103,24 @@
         pa=send(own.at[top], own.at[top], x_at(1)),
         mb=send(own.at[bottom], own.at[bottom], x_at(-1)),
         cp=send(own, own, partner),
+    )
+
+    for copy in row_near + column_near:
+        copy.wait_recv()
+    passed_ids = ids_all.at[z * RING + ring(y, -1)]
+    row_far = send(passed_ids, passed_ids, y_at(1))
+    column_far = send(column_ids.at[0], column_ids.at[2], z_at(1))
+
+    for h in range(2):
+        cols = pl.ds(h * wide, wide)
+        near = lines[h][0]
+        moved[h].update(
+            pb=send(pts_hbm.at[last, cols], gathered.at[h, 0, last], near(1)),
+            ma=send(pts_hbm.at[first, cols], gathered.at[h, 1, first], near(-1)),
+        )
+    tab.update(
+        pb=send(own.at[bottom], own.at[bottom], x_at(1)),
+        ma=send(own.at[top], own.at[top], x_at(-1)),
     )
 
     fetches[4].wait()
@@ -129,18 +143,6 @@
 
     lax.fori_loop(0, pts.shape[0] // 64, norm_points, 0)
 
-    for h in range(2):
-        cols = pl.ds(h * wide, wide)
-        near = lines[h][0]
-        moved[h].update(
-            pb=send(pts_hbm.at[last, cols], gathered.at[h, 0, last], near(1)),
-            ma=send(pts_hbm.at[first, cols], gathered.at[h, 1, first], near(-1)),
-        )
-    tab.update(
-        pb=send(own.at[bottom], own.at[bottom], x_at(1)),
-        ma=send(own.at[top], own.at[top], x_at(-1)),
-    )
-
     def score(slot):
         def step(i, carry):
             at = pl.ds(pl.multiple_of(i * 256, 256), 256)
@@ -154,12 +156,6 @@
 
         lax.fori_loop(0, pts.shape[0] // 256, step, 0)
 
-    fetches[2].wait()
-    for copy in id_near:
-        copy.wait_recv()
-    passed_ids = ids_all.at[z * RING + ring(y, -1)]
-    id_far = send(passed_ids, passed_ids, y_at(1))
-
     own_rows = part.shape[2]
     group_base = dp * (RING * RING * own_rows)
 
@@ -167,11 +163,13 @@
         at = (ring(z, d) * RING + y) if h == 0 else (z * RING + ring(y, d))
         return group_base + at * own_rows
 
-    def source_at(h, step):
-        return (z * RING + ring(y, step)) if h == 0 else (ring(z, step) * RING + y)
+    def ids_of(h, step):
+        if h == 0 or step == 0:
+            return ids_all.at[z * RING + ring(y, step)]
+        return column_ids.at[{-1: 0, 1: 1, 2: 2}[step]]
 
     def accumulate(h, step, points, lo, fresh=False):
-        ids = ids_all[source_at(h, step), :, lo:lo + half]
+        ids = ids_of(h, step)[:, lo:lo + half]
         for d in range(RING):
             target = lax.broadcasted_iota(jnp.int32, (own_rows, half), 0) + owner_base(h, d)
             onehot[d * own_rows:(d + 1) * own_rows] = jnp.where(target == ids, 1.0, 0.0).astype(BF16)
@@ -185,7 +183,7 @@
                     part[2 * k + h, d] += piece
 
     def prepare(h):
-        ids = ids_all[source_at(h, 2)]
+        ids = ids_of(h, 2)[...]
         for d in range(RING):
             target = lax.broadcasted_iota(jnp.int32, (own_rows, 2 * half), 0) + owner_base(h, d)
             across_hot[h, d] = jnp.where(target == ids, 1.0, 0.0).astype(BF16)
@@ -195,22 +193,12 @@
             across_hot[h, d], gathered[h, 2, :, k * part_w:(k + 1) * part_w], preferred_element_type=F32
         )
 
-    cols = slice(0, wide), slice(wide, 2 * wide)
-    accumulate(0, 0, pts[0:half, cols[0]], 0, fresh=True)
-    accumulate(0, 0, pts[half:, cols[0]], half)
-    id_far.wait_recv()
-    rows_ids = ids_all.at[pl.ds(z * RING, RING)]
-    id_near = [send(rows_ids, rows_ids, z_at(1)), send(rows_ids, rows_ids, z_at(-1))]
+    fetches[2].wait()
+    for h in range(2):
+        cols = slice(h * wide, (h + 1) * wide)
+        accumulate(h, 0, pts[0:half, cols], 0, fresh=True)
+        accumulate(h, 0, pts[half:, cols], half)
     score(dp)
-    tab["cp"].wait_recv()
-    other = 1 - core
-    score(x * 2 + other)
-    for copy in id_near:
-        copy.wait_recv()
-    passed_ids = ids_all.at[pl.ds(ring(z, -1) * RING, RING)]
-    id_far = send(passed_ids, passed_ids, z_at(1))
-    accumulate(1, 0, pts[0:half, cols[1]], 0, fresh=True)
-    accumulate(1, 0, pts[half:, cols[1]], half)
 
     def pass_points(h, k):
         near = lines[h][0]
@@ -218,36 +206,31 @@
         moved[h]["fa", k] = send(gathered.at[h, 0, first, cols], gathered.at[h, 2, first, cols], near(1))
         moved[h]["fb", k] = send(gathered.at[h, 1, last, cols], gathered.at[h, 2, last, cols], near(-1))
 
+    row_far.wait_recv()
+    rows_ids = ids_all.at[pl.ds(z * RING, RING)]
+    rows_near = [send(rows_ids, rows_ids, z_at(1)), send(rows_ids, rows_ids, z_at(-1))]
     for h in range(2):
         moved[h]["pa"].wait_recv()
         moved[h]["mb"].wait_recv()
-        pass_points(h, 0)
+        for k in range(2):
+            pass_points(h, k)
     before = table.at[ring(x, -1) * 2 + core]
     after = table.at[ring(x, 1) * 2 + core]
     across = table.at[ring(x, 2) * 2 + core]
-    for h in range(2):
-        accumulate(h, -1, gathered[h, 0, 0:half], 0)
-        accumulate(h, 1, gathered[h, 1, half:], half)
-    for h in range(2):
-        pass_points(h, 1)
     tab["pa"].wait_recv()
     tab["fa"] = send(before.at[top], before.at[top], x_at(1))
     tab["mb"].wait_recv()
     tab["fb"] = send(after.at[bottom], after.at[bottom], x_at(-1))
-    id_far.wait_recv()
-
-    def count(i, carry):
-        target = lax.broadcasted_iota(jnp.int32, (own_rows, BLOCK), 0) + (group_base + cent * own_rows)
-        for j in range(ids_all.shape[2] // BLOCK):
-            carry = carry + jnp.where(target == ids_all[i, :, j * BLOCK:(j + 1) * BLOCK], 1.0, 0.0)
-        return carry
-
-    counts = lax.fori_loop(0, ids_all.shape[0], count, jnp.zeros((own_rows, BLOCK), F32))
-    counts = jnp.maximum(jnp.sum(counts, axis=1, keepdims=True), 1.0)
-
-    inverse = 1.0 / counts
-    block = up.shape[2]
-    sub = block // RING
+    column_far.wait_recv()
+    for h in range(2):
+        accumulate(h, -1, gathered[h, 0, 0:half], 0)
+        accumulate(h, 1, gathered[h, 1, half:], half)
+
+    tab["cp"].wait_recv()
+    other = 1 - core
+    score(x * 2 + other)
+    sub = up.shape[3]
+    block = sub * RING
     local = parent_ref[...] - dp * (RING * block)
     swapped = (
         lax.shift_right_logical(local & (block - 1), 5) * block
@@ -272,6 +255,11 @@
     tab["ma"].wait_recv()
     tab["q1"] = send(after, after, partner)
 
+    for copy in rows_near:
+        copy.wait_recv()
+    passed_ids = ids_all.at[pl.ds(ring(z, -1) * RING, RING)]
+    rows_far = send(passed_ids, passed_ids, z_at(1))
+
     class Scatter:
         def __init__(self, src, f, q, line):
             self.src, self.f, self.q, self.line = src, f, q, line
@@ -281,10 +269,6 @@
             a, b = pl.ds(0, self.n), pl.ds(self.n, self.n)
             self.c2a = send(self.src(2).at[a], self.f.at[0], self.line(1))
             self.c2b = send(self.src(2).at[b], self.f.at[1], self.line(-1))
-
-        def left(self):
-            sent(self.c2a)
-            sent(self.c2b)
 
         def near(self):
             a, b = pl.ds(0, self.n), pl.ds(self.n, self.n)
@@ -321,26 +305,28 @@
         for h in range(2):
             finish(h, k, 1)
             finish(h, k, 3)
-            if k == 0:
-                sums[h].near()
+            sums[2 * k + h].near()
         for h in range(2):
             finish(h, k, 0)
         score(ring(x, -1 + 2 * k) * 2 + core)
-    sums[2].near()
-    sums[3].near()
     sums[0].forward()
     sums[1].forward()
     tab["fa"].wait_recv()
     tab["fb"].wait_recv()
     tab["q2"] = send(across, across, partner)
-    tab["q0"].wait_recv()
-    score(ring(x, -1) * 2 + other)
     sums[2].forward()
     sums[3].forward()
-    tab["q1"].wait_recv()
-    score(ring(x, 1) * 2 + other)
-    score(ring(x, 2) * 2 + core)
-    tab["q2"].wait_recv()
+    rows_far.wait_recv()
+    def count(i, carry):
+        target = lax.broadcasted_iota(jnp.int32, (own_rows, BLOCK), 0) + (group_base + cent * own_rows)
+        for j in range(ids_all.shape[2] // BLOCK):
+            carry = carry + jnp.where(target == ids_all[i, :, j * BLOCK:(j + 1) * BLOCK], 1.0, 0.0)
+        return carry
+
+    counts = lax.fori_loop(0, ids_all.shape[0], count, jnp.zeros((own_rows, BLOCK), F32))
+    counts = jnp.maximum(jnp.sum(counts, axis=1, keepdims=True), 1.0)
+
+    inverse = 1.0 / counts
     fetches[3].wait()
     squares = jnp.zeros((own_rows, 1), F32)
     for g in range(4):
@@ -351,54 +337,78 @@
     scale = lax.rsqrt(squares / pts.shape[1] + EPSILON)
 
     his, los = [], []
-    for g in range(4):
-        values = c1_ref[:, columns(g)] * scale
-        c1_ref[:, columns(g)] = values
+    for h in range(2):
+        values = c1_ref[:, h * wide:(h + 1) * wide] * scale
+        c1_ref[:, h * wide:(h + 1) * wide] = values
         hi = values.astype(BF16)
         his.append(hi)
         los.append((values - hi.astype(F32)).astype(BF16))
 
-    def upper(g, d):
-        pick = picks[g % 2, d]
-        up[g, d] = jnp.dot(pick, his[g], preferred_element_type=F32) + jnp.dot(
-            pick, los[g], preferred_element_type=F32
+    def upper(h, d):
+        pick = picks[h, d]
+        sums = jnp.dot(pick, his[h], preferred_element_type=F32) + jnp.dot(
+            pick, los[h], preferred_element_type=F32
         )
-
-    ups = scatter(lambda g, d: up.at[g, d], up_f, up_q, 1)
-    for g in range(4):
-        upper(g, 2)
-        ups[g].far()
-    for g in range(4):
-        upper(g, 1)
-        upper(g, 3)
-    for g in range(4):
-        ups[g].left()
-        ups[g].near()
-    for g in range(4):
-        upper(g, 0)
-    for g in range(4):
-        ups[g].forward()
-    score(ring(x, 2) * 2 + other)
-    totals = jnp.sum(score_acc[...], axis=0, keepdims=True)
-    for b in range(pts.shape[0] // BLOCK):
-        score_ref[b:b + 1, :] = jnp.log(totals[:, b * BLOCK:(b + 1) * BLOCK])
-    lows = scatter(lambda g, d: low.at[g, ring(me[g % 2][1], d)], low_f, low_q, 0)
-    for g in range(4):
-        ups[g].wait()
-        low[g] = (up[g, 0] + up_q[g, 0] + up_q[g, 1]).reshape(RING, sub, part_w)
-        lows[g].far()
-        lows[g].near()
-    for g in range(4):
-        lows[g].forward()
+        up[h, d] = sums.reshape(RING, sub, wide)
+
+    def scatter_up(h, step):
+        j = ring(me[h][1], step)
+        return Scatter(lambda d: up.at[h, d, j], up_f.at[h, step], up_q.at[h, step], lines[h][1])
+
+    def settle(h, step):
+        ups[h][step].wait()
+        j = ring(me[h][1], step)
+        low[h, j] = up[h, 0, j] + up_q[h, step, 0] + up_q[h, step, 1]
+
+    ups = [[scatter_up(h, step) for step in range(RING)] for h in range(2)]
+    lows = [
+        Scatter(lambda d, h=h: low.at[h, ring(me[h][1], d)], low_f.at[h], low_q.at[h], lines[h][0]) for h in range(2)
+    ]
+    for h in range(2):
+        upper(h, 2)
+        for step in (2, 1, 3, 0):
+            ups[h][step].far()
+    for h in range(2):
+        upper(h, 1)
+        upper(h, 3)
+        ups[h][2].near()
+    for h in range(2):
+        upper(h, 0)
+    for h in range(2):
+        ups[h][2].forward()
+    for h in range(2):
+        for step in (1, 3):
+            ups[h][step].near()
+    for h in range(2):
+        for step in (1, 3):
+            ups[h][step].forward()
+    for h in range(2):
+        ups[h][0].near()
+        ups[h][0].forward()
+    tab["q0"].wait_recv()
+    score(ring(x, -1) * 2 + other)
+    for h in range(2):
+        settle(h, 2)
+        lows[h].far()
+    for h in range(2):
+        settle(h, 1)
+        settle(h, 3)
+        lows[h].near()
+    for h in range(2):
+        lows[h].forward()
+    tab["q1"].wait_recv()
+    score(ring(x, 1) * 2 + other)
+    for h in range(2):
+        settle(h, 0)
     squares = jnp.zeros((sub, 1), F32)
     values = []
-    for g in range(4):
-        lows[g].wait()
-        values.append(low[g, me[g % 2][1]] + low_q[g, 0] + low_q[g, 1])
-        squares = squares + jnp.sum(values[g] * values[g], axis=1, keepdims=True)
+    for h in range(2):
+        lows[h].wait()
+        values.append(low[h, me[h][1]] + low_q[h, 0] + low_q[h, 1])
+        squares = squares + jnp.sum(values[h] * values[h], axis=1, keepdims=True)
     scale = lax.rsqrt(squares / pts.shape[1] + EPSILON)
-    for g in range(4):
-        c2_ref[z, y, :, columns(g)] = values[g] * scale
+    for h in range(2):
+        c2_ref[z, y, :, h * wide:(h + 1) * wide] = values[h] * scale
 
     def piece(h, i, j, rows=pl.ds(0, sub)):
         at = (i, j) if h == 0 else (j, i)
@@ -409,6 +419,11 @@
     def spread(h, i, j, line):
         src = piece(h, i, j)
         return send(src, src, line(1)), send(src, src, line(-1))
+
+    def spread_halves(h, i, j, line):
+        high, low_rows = piece(h, i, j, upper_half), piece(h, i, j, lower_half)
+        first_pair = send(high, high, line(1)), send(low_rows, low_rows, line(-1))
+        return first_pair + (send(low_rows, low_rows, line(1)), send(high, high, line(-1)))
 
     def pass_on(pair, low_src, high_src, line):
         pair[0].wait_recv()
@@ -425,13 +440,11 @@
     near_pairs, far_pairs, passed = [], [], []
     for h in range(2):
         i, j = me[h]
-        near_pairs.append(spread(h, i, j, lines[h][0]))
-    for h in range(2):
-        for copy in near_pairs[h]:
-            sent(copy)
+        near_pairs.append(spread_halves(h, i, j, lines[h][0]))
     for h in range(2):
         i, j = me[h]
         far_pairs.append({0: spread(h, i, j, lines[h][1])})
+    score(ring(x, 2) * 2 + core)
     crossed = []
     for h in range(2):
         i, j = me[h]
@@ -440,27 +453,36 @@
         ))
     for h in range(2):
         i, j = me[h]
+        near_pairs[h][2].wait_recv()
         far_pairs[h][-1] = spread(h, i, ring(j, -1), lines[h][1])
+        near_pairs[h][3].wait_recv()
         far_pairs[h][1] = spread(h, i, ring(j, 1), lines[h][1])
     for h in range(2):
         passed.append(pass_far(h, me[h][1], far_pairs[h][0]))
+    tab["q2"].wait_recv()
+    score(ring(x, 2) * 2 + other)
     for h in range(2):
         i, j = me[h]
         for copy in crossed[h]:
             copy.wait_recv()
-        far_pairs[h][2] = spread(h, i, ring(j, 2), lines[h][1])
+        far_pairs[h][2] = spread_halves(h, i, ring(j, 2), lines[h][1])
     for step in (-1, 1, 2):
         for h in range(2):
             passed.append(pass_far(h, ring(me[h][1], step), far_pairs[h][step]))
+    for h in range(2):
+        passed.append(far_pairs[h][2][2:])
+    totals = jnp.sum(score_acc[...], axis=0, keepdims=True)
+    for b in range(pts.shape[0] // BLOCK):
+        score_ref[b:b + 1, :] = jnp.log(totals[:, b * BLOCK:(b + 1) * BLOCK])
     for pair in passed:
         for copy in pair:
             copy.wait_recv()
-    for copy in pending:
+    for copy in copies:
         copy.wait_send()
     assert len(copies) == N_COPIES
 
 
-N_COPIES = 144
+N_COPIES = 167
 
 
 def shards(points, point_cluster, cand_blocks, cent1_prev, parent, cent2_prev):
@@ -499,12 +521,13 @@
             pltpu.VMEM((4, 2, owned // 2, wide // 2), F32),
             pltpu.VMEM((4, 2, owned, wide // 2), F32),
             pltpu.VMEM((owned, width), F32),
-            pltpu.VMEM((4, RING, block, wide // 2), F32),
-            pltpu.VMEM((4, 2, block // 2, wide // 2), F32),
-            pltpu.VMEM((4, 2, block, wide // 2), F32),
-            pltpu.VMEM((4, RING, sub, wide // 2), F32),
-            pltpu.VMEM((4, 2, sub // 2, wide // 2), F32),
-            pltpu.VMEM((4, 2, sub, wide // 2), F32),
+            pltpu.VMEM((2, RING, RING, sub, wide), F32),
+            pltpu.VMEM((2, RING, 2, sub // 2, wide), F32),
+            pltpu.VMEM((2, RING, 2, sub, wide), F32),
+            pltpu.VMEM((2, RING, sub, wide), F32),
+            pltpu.VMEM((2, 2, sub // 2, wide), F32),
+            pltpu.VMEM((2, 2, sub, wide), F32),
+            pltpu.VMEM((3, 1, rows), jnp.int32),
             pltpu.SMEM(cand_blocks.shape, jnp.int32),
             pltpu.VMEM((1, owned), jnp.int32),
             pltpu.SemaphoreType.DMA((N_COPIES,)),

time: 105 us -> 98.3 us (0.936)
  Pallas kernels: 102 us -> 94.6 us
    pallas_call x1, Pallas kernels: 102 us -> 94.6 us  [shards(): pl.pallas_call(kernel, out_shape=(jax.ShapeDtypeStruct((owned, width), F3...]
where the time goes in v3:
time: 98.3 us; the launch traced here: 98.1 us
  Pallas kernels  94.6 us (96%)
  local copies, waits for them, and re-layouts  2.88 us (3%)
    pallas_call x1, Pallas kernels, shards(): pl.pallas_call(kernel, out_shape=(jax.ShapeDtypeStruct((owned, width), F3...  94.6 us
    unnamed x3, local copies, waits for them, and re-layouts  2.88 us

profile of v3, /device:TPU:0, one launch (start us, length us, event | category | flops | bytes accessed | tf_op | source)
XLA Modules:
  0.0 98.1 jit_solution(17682742048417331844)
XLA Ops:
  0.6 94.6 %shard_map.85 = (f32[256,1024]{1,0:T(8,128)S(1)}, f32[4,4,32,1024]{3,2,1,0:T(8,128)S(1)}, f32[8,128]{1,0:T(8,128)S(1)}) custom-call(bf16[1024,1024]{1,0:T(8,128)(2,1)} %pts_hbm.1, s32[1,1024]{1,0:T(1,128)} %bitcast.6, s32[8,8]{1,0:T(8,128)} %cand_hbm.1, f32[256,1024]{1,0:T(8,128)} %prev_hbm.1, s32[1,256]{1,0:T(1,128)} %bitcast.7, bf16[512,1024]{1,0:T(8,128)(2,1)} %tab_hbm.1), custom_call_target="tpu_custom_call" | custom-call | tf_op jit(solution)/shard_map/pallas_call | solution.py:499
  95.3 1.0 copy.12
  96.2 1.3 %copy.13 = f32[512,1024]{1,0:T(8,128)} copy(f32[512,1024]{1,0:T(8,128)S(1)} %bitcast.4) | data formatting | bytes 4194304
  97.6 0.6 copy.14

commit v4 on v3

--- a/solution.py
+++ b/solution.py
@@ -316,6 +316,8 @@
     tab["q2"] = send(across, across, partner)
     sums[2].forward()
     sums[3].forward()
+    tab["q0"].wait_recv()
+    score(ring(x, -1) * 2 + other)
     rows_far.wait_recv()
     def count(i, carry):
         target = lax.broadcasted_iota(jnp.int32, (own_rows, BLOCK), 0) + (group_base + cent * own_rows)
@@ -385,8 +387,6 @@
     for h in range(2):
         ups[h][0].near()
         ups[h][0].forward()
-    tab["q0"].wait_recv()
-    score(ring(x, -1) * 2 + other)
     for h in range(2):
         settle(h, 2)
         lows[h].far()
@@ -483,6 +483,22 @@
 
 
 N_COPIES = 167
+N_PIECES = 4
+
+
+def put_out(*refs):
+    sources, targets, sem = refs[:3], refs[3:6], refs[6]
+    moves = []
+    for k, (source, target) in enumerate(zip(sources, targets)):
+        pieces = N_PIECES if k < 2 else 1
+        step = source.shape[0] // pieces
+        for i in range(pieces):
+            rows = pl.ds(i * step, step)
+            moves.append(pltpu.make_async_copy(source.at[rows], target.at[rows], sem.at[k, i]))
+    for move in moves:
+        move.start()
+    for move in moves:
+        move.wait()
 
 
 def shards(points, point_cluster, cand_blocks, cent1_prev, parent, cent2_prev):
@@ -545,6 +561,15 @@
         pltpu.with_memory_space_constraint(parent.reshape(1, owned), pltpu.HBM),
         pltpu.with_memory_space_constraint(cent2_prev, pltpu.HBM),
     )
+    results = (cent1_new, cent2_new, score)
+    cent1_new, cent2_new, score = pl.pallas_call(
+        put_out,
+        out_shape=tuple(jax.ShapeDtypeStruct(r.shape, r.dtype) for r in results),
+        in_specs=[vmem] * 3,
+        out_specs=(hbm,) * 3,
+        scratch_shapes=[pltpu.SemaphoreType.DMA((3, N_PIECES))],
+        compiler_params=pltpu.CompilerParams(vmem_limit_bytes=16 * 1024 * 1024),
+    )(*results)
     return cent1_new, cent2_new.reshape(table_rows, width), score.reshape(rows)
 
 

time: 98.3 us -> 97 us (0.987)
  local copies, waits for them, and re-layouts: 2.88 us -> 0 us
  Pallas kernels: 94.6 us -> 96.1 us
    unnamed x3 -> x0, local copies, waits for them, and re-layouts: 2.88 us -> none
    pallas_call x0 -> x1, Pallas kernels: none -> 1.77 us  [shards(): pl.pallas_call(put_out, out_shape=tuple((jax.ShapeDtypeStruct(r.shape, r....]
where the time goes in v4:
time: 97 us; the launch traced here: 96.9 us
  Pallas kernels  96.1 us (99%)
    pallas_call x1, Pallas kernels, shards(): pl.pallas_call(kernel, out_shape=(jax.ShapeDtypeStruct((owned, width), F3...  94.3 us

profile of v4, /device:TPU:0, one launch (start us, length us, event | category | flops | bytes accessed | tf_op | source)
XLA Modules:
  0.0 96.9 jit_solution(7868775317355991906)
XLA Ops:
  0.6 94.3 %shard_map.85 = (f32[256,1024]{1,0:T(8,128)S(1)}, f32[4,4,32,1024]{3,2,1,0:T(8,128)S(1)}, f32[8,128]{1,0:T(8,128)S(1)}) custom-call(bf16[1024,1024]{1,0:T(8,128)(2,1)} %pts_hbm.1, s32[1,1024]{1,0:T(1,128)} %bitcast.4, s32[8,8]{1,0:T(8,128)} %cand_hbm.1, f32[256,1024]{1,0:T(8,128)} %prev_hbm.1, s32[1,256]{1,0:T(1,128)} %bitcast.5, bf16[512,1024]{1,0:T(8,128)(2,1)} %tab_hbm.1), custom_call_target="tpu_custom_call" | custom-call | tf_op jit(solution)/shard_map/pallas_call | solution.py:515
  94.9 1.8 %shard_map.86 = (f32[256,1024]{1,0:T(8,128)}, f32[4,4,32,1024]{3,2,1,0:T(8,128)}, f32[8,128]{1,0:T(8,128)}) custom-call(f32[256,1024]{1,0:T(8,128)S(1)} %get-tuple-element.9.refs_0_, f32[4,4,32,1024]{3,2,1,0:T(8,128)S(1)} %get-tuple-element.10.refs_1_, f32[8,128]{1,0:T(8,128)S(1)} %get-tuple-element.11.refs_2_), custom_call_target="tpu_custom_call" | custom-call | tf_op jit(solution)/shard_map/pallas_call | solution.py:565

commit v5 on v4

--- a/solution.py
+++ b/solution.py
@@ -339,12 +339,6 @@
     scale = lax.rsqrt(squares / pts.shape[1] + EPSILON)
 
     his, los = [], []
-    for h in range(2):
-        values = c1_ref[:, h * wide:(h + 1) * wide] * scale
-        c1_ref[:, h * wide:(h + 1) * wide] = values
-        hi = values.astype(BF16)
-        his.append(hi)
-        los.append((values - hi.astype(F32)).astype(BF16))
 
     def upper(h, d):
         pick = picks[h, d]
@@ -367,6 +361,11 @@
         Scatter(lambda d, h=h: low.at[h, ring(me[h][1], d)], low_f.at[h], low_q.at[h], lines[h][0]) for h in range(2)
     ]
     for h in range(2):
+        values = c1_ref[:, h * wide:(h + 1) * wide] * scale
+        c1_ref[:, h * wide:(h + 1) * wide] = values
+        hi = values.astype(BF16)
+        his.append(hi)
+        los.append((values - hi.astype(F32)).astype(BF16))
         upper(h, 2)
         for step in (2, 1, 3, 0):
             ups[h][step].far()

time: 97 us -> 97.1 us (level)
  no operation moved by 1% of the time
where the time goes in v5:
time: 97.1 us; the launch traced here: 97 us
  Pallas kernels  96.2 us (99%)
    pallas_call x1, Pallas kernels, shards(): pl.pallas_call(kernel, out_shape=(jax.ShapeDtypeStruct((owned, width), F3...  94.4 us

profile of v5, /device:TPU:0, one launch (start us, length us, event | category | flops | bytes accessed | tf_op | source)
XLA Modules:
  0.0 97.0 jit_solution(8050789237106607397)
XLA Ops:
  0.6 94.4 %shard_map.85 = (f32[256,1024]{1,0:T(8,128)S(1)}, f32[4,4,32,1024]{3,2,1,0:T(8,128)S(1)}, f32[8,128]{1,0:T(8,128)S(1)}) custom-call(bf16[1024,1024]{1,0:T(8,128)(2,1)} %pts_hbm.1, s32[1,1024]{1,0:T(1,128)} %bitcast.4, s32[8,8]{1,0:T(8,128)} %cand_hbm.1, f32[256,1024]{1,0:T(8,128)} %prev_hbm.1, s32[1,256]{1,0:T(1,128)} %bitcast.5, bf16[512,1024]{1,0:T(8,128)(2,1)} %tab_hbm.1), custom_call_target="tpu_custom_call" | custom-call | tf_op jit(solution)/shard_map/pallas_call | solution.py:514
  95.1 1.8 %shard_map.86 = (f32[256,1024]{1,0:T(8,128)}, f32[4,4,32,1024]{3,2,1,0:T(8,128)}, f32[8,128]{1,0:T(8,128)}) custom-call(f32[256,1024]{1,0:T(8,128)S(1)} %get-tuple-element.9.refs_0_, f32[4,4,32,1024]{3,2,1,0:T(8,128)S(1)} %get-tuple-element.10.refs_1_, f32[8,128]{1,0:T(8,128)S(1)} %get-tuple-element.11.refs_2_), custom_call_target="tpu_custom_call" | custom-call | tf_op jit(solution)/shard_map/pallas_call | solution.py:564
